TPU v7x, 32 devices: a whole 2x2x4 slice. The times are simulated.
32 devices in a mesh: groups: 2 (over x), grid: 16 (over z, y, core).
Axes of the slice: x: 2, y: 2, z: 4, core: 2. Of those that a mesh axis runs over, the one named last changes fastest.
Arguments:
- hist: float32 [768, 256, 256], P('groups', 'grid'), parts along dimension 0, may hold values from 0.2 to 2
- drift: float32 [2, 256, 256], P(None, 'grid'), may hold values from -0.5 to 0.5
- shocks: int32 [768, 2], P('groups'), parts along dimension 0, may hold values from 0 to 7
- shock_table: float32 [16, 2], P('groups'), parts along dimension 0, may hold values from -0.3 to 0.3
- first_weight: bfloat16 [131072, 2048], P(('groups', 'grid')), parts along dimension 0, may hold values from -0.03125 to 0.03125
- mid_weight: bfloat16 [4096, 2048], P('groups', 'grid'), parts along dimension 0, may hold values from -0.1875 to 0.1875
- head_weight: float32 [4096], P(('groups', 'grid')), parts along dimension 0, may hold values from -0.125 to 0.125
- cotangent: float32 [768], P('groups'), parts along dimension 0, may hold values from -6 to 6
Outputs:
- hist_next: float32 [768, 256, 256], P('groups', 'grid'), parts along dimension 0
- value: float32 [768], P('groups'), parts along dimension 0
- grad_first: bfloat16 [131072, 2048], P(('groups', 'grid')), parts along dimension 0
- grad_mid: bfloat16 [4096, 2048], P('groups', 'grid'), parts along dimension 0
- grad_head: float32 [4096], P(('groups', 'grid')), parts along dimension 0
There are 2 independent parts, one for each index of `groups`. A program takes and returns all parts, laid end to end along the dimension named above; an argument that names none is the same for every part. Nothing has to cross between parts.
All inputs are finite; a program needn't handle non-finite values.
Results may differ from a plain program's by a relative error of at most 0.0173.
Values may be sent and summed in bfloat16 or wider, within the bound.
A program may use at most 128 MiB of HBM per device.

v0:
```python
import jax
import jax.numpy as jnp
from jax import lax
from jax.sharding import PartitionSpec as P

diffusion_rate = 0.24


def padded_2(block, sides, width):
    for axis, dim in sides:
        count = lax.axis_size(axis)
        forward = [(i, i + 1) for i in range(count - 1)]
        backward = [(target, source) for source, target in forward]
        low = lax.ppermute(
            lax.slice_in_dim(block, block.shape[dim] - width, None, axis=dim), axis, forward
        )
        high = lax.ppermute(lax.slice_in_dim(block, 0, width, axis=dim), axis, backward)
        block = jnp.concatenate([low, block, high], axis=dim)
    return block


def column_shift(values, offset):
    zero_col = jnp.zeros_like(values[..., :1])
    if offset > 0:
        return jnp.concatenate([values[..., 1:], zero_col], axis=-1)
    return jnp.concatenate([zero_col, values[..., :-1]], axis=-1)


def shock_shift(levels_now, table):
    level_ids = lax.iota(jnp.int32, table.shape[0])
    onehot = (levels_now[:, None] == level_ids[None, :]).astype(jnp.float32)
    return jnp.sum(onehot[:, :, None] * table[None, :, :], axis=1)


def kfe_step(padded, drift_rows, shift_x, shift_y):
    velocity_x = drift_rows[0][None] + shift_x[:, None, None]
    velocity_y = drift_rows[1][1:-1][None] + shift_y[:, None, None]
    flux_x = velocity_x * padded
    centre = padded[:, 1:-1]
    flux_y = velocity_y * centre
    spread = (
        padded[:, 2:]
        + padded[:, :-2]
        + column_shift(centre, 1)
        + column_shift(centre, -1)
        - 4.0 * centre
    )
    carried = 0.5 * (flux_x[:, 2:] - flux_x[:, :-2]) + 0.5 * (
        column_shift(flux_y, 1) - column_shift(flux_y, -1)
    )
    return centre + diffusion_rate * spread - carried


def local(hist, drift, shocks, shock_table, first_weight, mid_weight, head_weight, cotangent):
    scenarios, row_count, columns = hist.shape
    step_count = shocks.shape[1]
    density = hist
    drift_ext = padded_2(drift, (("grid", 1),), 1)
    for section_no in range(step_count):
        shifts = shock_shift(shocks[:, section_no], shock_table)
        padded = padded_2(density, (("grid", 1),), 1)
        density = kfe_step(padded, drift_ext, shifts[:, 0], shifts[:, 1])
    inputs = density.astype(jnp.bfloat16).reshape(scenarios, row_count * columns)
    partial_first = jnp.dot(inputs, first_weight, preferred_element_type=jnp.float32)
    first_pre = lax.psum(partial_first, "grid")
    first_act = jnp.tanh(first_pre).astype(jnp.bfloat16)
    second_pre = jnp.dot(first_act, mid_weight, preferred_element_type=jnp.float32)
    second_act = jnp.tanh(second_pre).astype(jnp.bfloat16)
    second_f = second_act.astype(jnp.float32)
    value_part = jnp.dot(second_f, head_weight, precision=lax.Precision.HIGHEST)
    value = lax.psum(value_part, "grid")
    grad_head = jnp.dot(cotangent, second_f, precision=lax.Precision.HIGHEST)
    back_second = (cotangent[:, None] * head_weight[None, :] * (1.0 - second_f * second_f)).astype(
        jnp.bfloat16
    )
    grad_mid = lax.dot_general(
        first_act, back_second, (((0,), (0,)), ((), ())), preferred_element_type=jnp.float32
    )
    back_part = lax.dot_general(
        back_second, mid_weight, (((1,), (1,)), ((), ())), preferred_element_type=jnp.float32
    )
    back_raw = lax.psum(back_part, "grid")
    first_f = first_act.astype(jnp.float32)
    back_first = (back_raw * (1.0 - first_f * first_f)).astype(jnp.bfloat16)
    grad_first = lax.dot_general(
        inputs, back_first, (((0,), (0,)), ((), ())), preferred_element_type=jnp.float32
    )
    return (
        density,
        value,
        grad_first.astype(jnp.bfloat16),
        grad_mid.astype(jnp.bfloat16),
        grad_head,
    )


def solution(mesh):
    in_specs = (
        P("groups", "grid", None),
        P(None, "grid", None),
        P("groups", None),
        P("groups", None),
        P(("groups", "grid"), None),
        P("groups", "grid"),
        P(("groups", "grid")),
        P("groups"),
    )
    out_specs = (
        P("groups", "grid", None),
        P("groups"),
        P(("groups", "grid"), None),
        P("groups", "grid"),
        P(("groups", "grid")),
    )
    return jax.shard_map(local, mesh=mesh, in_specs=in_specs, out_specs=out_specs, check_vma=False)
```

profile of v0, /device:TPU:0, one launch (start us, length us, event | category | flops | bytes accessed | tf_op | source)
XLA Modules:
  0.0 387.2 jit_solution(2880481211151766229)
XLA Ops:
  7.2 0.8 fusion.37
  8.0 2.4 collective-permute-start.2
  10.4 1.3 collective-permute-start.3
  11.7 3.4 fusion.35
  15.1 1.3 collective-permute-start
  17.2 6.7 %collective-permute-start.1 = (f32[384,1,256]{2,0,1:T(8,128)}, f32[384,1,256]{2,0,1:T(8,128)}, u32[]{:S(2)}, u32[]{:S(2)}) collective-permute-start(f32[384,1,256]{2,0,1:T(8,128)} %copy.71), channel_id=1, source_target_pairs={{0,1},{1,2},{2,3},{3,4},{4,5},{5,6},{6,7},{7,8},{8,9},{9,10},{10,1... | collective-permute-start | bytes 1179656 | tf_op jit(solution)/shard_map/ppermute | solution.py:14
  23.9 6.6 %copy.58 = f32[384,16,256]{0,2,1:T(8,128)} copy(f32[384,16,256]{2,1,0:T(8,128)} %param.8) | data formatting | bytes 12582912 | tf_op args[0]
  30.7 10.8 %fusion.34 = (f32[384,16,255]{0,2,1:T(8,128)}, f32[384,16,255]{0,2,1:T(8,128)}) fusion(f32[384,16,256]{0,2,1:T(8,128)} %copy.58), kind=kLoop, calls=%fused_computation.63 | loop fusion | bytes 25067520 | tf_op jit(solution)/shard_map/slice | solution.py:25
  41.4 4.9 %add_multiply_fusion.1 = f32[384,16,256]{0,2,1:T(8,128)} fusion(f32[384,16,256]{0,2,1:T(8,128)} %copy.58, f32[384]{0:T(512)S(1)} %get-tuple-element.24, f32[16,256]{1,0:T(8,128)S(1)} %slice_bitcast_fusion), kind=kLoop, calls=%fused_computation.28 | loop fusion | flops 3145728 | bytes 12600832 | tf_op jit(solution)/shard_map/mul | solution.py:40
  46.4 10.8 %fusion.36 = (f32[384,16,255]{0,2,1:T(8,128)}, f32[384,16,255]{0,2,1:T(8,128)}) fusion(f32[384,16,256]{0,2,1:T(8,128)} %add_multiply_fusion.1), kind=kLoop, calls=%fused_computation.65 | loop fusion | bytes 25067520 | tf_op jit(solution)/shard_map/slice | solution.py:25
  57.4 1.3 copy.53
  58.7 6.0 %maximum_multiply_fusion = f32[384,18,256]{0,2,1:T(8,128)} fusion(f32[384,1,256]{0,2,1:T(8,128)S(1)} %copy.51, f32[384,16,256]{0,2,1:T(8,128)} %copy.58, f32[384,1,256]{0,2,1:T(8,128)S(1)} %copy.53, f32[384]{0:T(512)S(1)} %get-tuple-element.25, f32[18,256]{1,0:T(8,128)S(1)} %fusion.20), kind=kLoop, calls=%fused_computation.1 | loop fusion | flops 7077888 | bytes 14175744 | tf_op jit(solution)/shard_map/mul | solution.py:38
  64.8 2.4 slice-done.1
  67.2 14.2 %add_multiply_fusion = (f32[384,16,256]{0,2,1:T(8,128)}, f32[384,16,256]{0,2,1:T(8,128)S(1)}) fusion(f32[384]{0:T(512)S(1)} %get-tuple-element.20, f32[16,256]{1,0:T(8,128)S(1)} %slice_bitcast_fusion, f32[384,16,255]{0,2,1:T(8,128)} %get-tuple-element.43, f32[384,16,255]{0,2,1:T(8,128)} %get-tuple-element.42, f32[384,18,256]{0,2,1:T(8,128)} %maximum_multiply_fusion, ...), kind=kLoop, calls=%fused_computation.27 | loop fusion | flops 25165824 | bytes 57329152 | tf_op jit(solution)/shard_map/mul | solution.py:40
  81.4 2.6 copy-done.1
  84.1 10.8 %fusion.31 = (f32[384,16,255]{0,2,1:T(8,128)}, f32[384,16,255]{0,2,1:T(8,128)}) fusion(f32[384,16,256]{0,2,1:T(8,128)} %copy-done.1), kind=kLoop, calls=%fused_computation.60 | loop fusion | bytes 25067520 | tf_op jit(solution)/shard_map/slice | solution.py:25
  95.1 1.3 collective-permute-start.4
  96.5 4.3 %collective-permute-start.5 = (f32[384,1,256]{2,0,1:T(8,128)S(1)}, f32[384,1,256]{2,0,1:T(8,128)}, u32[]{:S(2)}, u32[]{:S(2)}) collective-permute-start(f32[384,1,256]{2,0,1:T(8,128)S(1)} %copy.65), channel_id=1, source_target_pairs={{0,1},{1,2},{2,3},{3,4},{4,5},{5,6},{6,7},{7,8},{8,9},{9,10},{10,1... | collective-permute-start | bytes 1179656 | tf_op jit(solution)/shard_map/ppermute | solution.py:14
  100.8 10.7 %fusion.33 = (f32[384,16,255]{0,2,1:T(8,128)}, f32[384,16,255]{0,2,1:T(8,128)}) fusion(f32[384,16,256]{0,2,1:T(8,128)} %get-tuple-element.30), kind=kLoop, calls=%fused_computation.62 | loop fusion | bytes 25067520 | tf_op jit(solution)/shard_map/slice | solution.py:25
  111.7 1.3 copy.66
  113.1 5.5 %maximum_multiply_fusion.1 = f32[384,18,256]{0,2,1:T(8,128)} fusion(f32[384,1,256]{0,2,1:T(8,128)S(1)} %copy.64, f32[384,16,256]{0,2,1:T(8,128)} %copy-done.1, f32[384,1,256]{0,2,1:T(8,128)S(1)} %copy.66, f32[384]{0:T(512)S(1)} %get-tuple-element.21, f32[18,256]{1,0:T(8,128)S(1)} %fusion.20), kind=kLoop, calls=%fused_computation.2 | loop fusion | flops 7077888 | bytes 14175744 | tf_op jit(solution)/shard_map/mul | solution.py:38
  118.7 17.3 %fusion.28 = (bf16[384,16,256]{0,2,1:T(8,128)(2,1)S(1)}, f32[384,16,256]{0,2,1:T(8,128)}) fusion(f32[384,16,255]{0,2,1:T(8,128)} %get-tuple-element.37, f32[384,16,255]{0,2,1:T(8,128)} %get-tuple-element.36, f32[384,18,256]{0,2,1:T(8,128)} %maximum_multiply_fusion.1, f32[384,16,256]{0,2,1:T(8,128)S(1)} %bitcast.21, f32[384,16,255]{0,2,1:T(8,128)} %get-tuple-element.33, ...), kind=kLoop, calls=%fused_computation.59 | loop fusion | flops 23592960 | bytes 54165504 | tf_op jit(solution)/shard_map/convert_element_type | solution.py:63
  136.0 1.7 copy-done.3
  137.7 12.1 %fusion.38 = f32[384,2048]{1,0:T(8,128)} fusion(bf16[384,4096]{0,1:T(8,128)(2,1)S(1)} %bitcast.22, bf16[4096,2048]{1,0:T(8,128)(2,1)} %param.12), kind=kOutput, calls=%fused_computation.67 | convolution fusion | flops 6442450944 | bytes 23068672 | tf_op jit(solution)/shard_map/dot_general | solution.py:64
  149.9 106.9 %all-reduce.11.cloned.1.call-done = f32[384,2048]{1,0:T(8,128)} async-done(((f32[384,2048]{1,0:T(8,128)}), f32[384,2048]{1,0:T(8,128)}) %all-reduce.11.cloned.1.call-update) | async-done | bytes 3145744 | tf_op jit(solution)/shard_map/psum | solution.py:65
  256.7 2.5 fusion.19
  259.2 2.3 fusion.23
  261.6 6.7 %copy.69 = f32[384,16,256]{2,1,0:T(8,128)} copy(f32[384,16,256]{0,2,1:T(8,128)} %get-tuple-element.29) | data formatting | bytes 12582912
  268.5 31.0 %psum.22 = f32[384]{0:T(512)} all-reduce(f32[384]{0:T(512)S(1)} %convolution_reduce_fusion), channel_id=1, replica_groups=mesh['groups'=2,'grid'=16] {'grid'}, use_global_device_ids=true, to_apply=%region_3.0 | all-reduce | flops 384 | bytes 3072 | tf_op jit(solution)/shard_map/psum | solution.py:71
  300.2 3.4 convolution_convert_fusion.1
  303.6 61.2 %all-reduce.13.cloned.1.call-done = f32[384,2048]{1,0:T(8,128)} async-done(((f32[384,2048]{1,0:T(8,128)}), f32[384,2048]{1,0:T(8,128)}) %all-reduce.13.cloned.1.call-update) | async-done | bytes 3145744 | tf_op jit(solution)/shard_map/psum | solution.py:82
  364.9 15.5 %convolution_convert_fusion = bf16[4096,2048]{1,0:T(8,128)(2,1)} fusion(bf16[384,4096]{0,1:T(8,128)(2,1)} %bitcast.23, f32[384,2048]{1,0:T(8,128)} %all-reduce.13.cloned.1.call-done, f32[384,2048]{1,0:T(8,128)} %all-reduce.11.cloned.1.call-done), kind=kOutput, calls=%fused_computation | convolution fusion | flops 6455558144 | bytes 26214400 | tf_op jit(solution)/shard_map/dot_general | solution.py:85
  (52 shorter events, 2.9 us)
Async XLA Ops:
  7.2 249.6 %copy-start = (bf16[2048,128]{1,0:T(8,128)(2,1)S(1)}, bf16[2048,128]{1,0:T(8,128)(2,1)}, u32[]{:S(2)}) copy-start(bf16[2048,128]{1,0:T(8,128)(2,1)} %param.13) | copy-start | bytes 1572868
  7.2 249.6 %all-reduce.11.cloned.1.call-start = ((), (), s32[]{:S(2)}) async-start(), calls=%async_computation | async-start | bytes 6291456 | tf_op jit(solution)/shard_map/psum | solution.py:65
  8.0 49.2 %collective-permute-start.2 = (f32[2,1,256]{2,1,0:T(1,128)S(1)}, f32[2,1,256]{2,1,0:T(1,128)S(1)}, u32[]{:S(2)}, u32[]{:S(2)}) collective-permute-start(f32[2,1,256]{2,1,0:T(1,128)S(1)} %get-tuple-element.44), channel_id=1, source_target_pairs={{0,1},{1,2},{2,3},{3,4},{4,5},{5,6},{6,7},{7,8},{8,9},{9,10},{10,1... | collective-permute-start | bytes 6152 | tf_op jit(solution)/shard_map/ppermute | solution.py:14
  10.4 46.8 %collective-permute-start.3 = (f32[2,1,256]{2,1,0:T(1,128)S(1)}, f32[2,1,256]{2,1,0:T(1,128)S(1)}, u32[]{:S(2)}, u32[]{:S(2)}) collective-permute-start(f32[2,1,256]{2,1,0:T(1,128)S(1)} %get-tuple-element.45), channel_id=1, source_target_pairs={{1,0},{2,1},{3,2},{4,3},{5,4},{6,5},{7,6},{8,7},{9,8},{10,9},{11,1... | collective-permute-start | bytes 6152 | tf_op jit(solution)/shard_map/ppermute | solution.py:17
  15.1 42.1 %collective-permute-start = (f32[384,1,256]{2,0,1:T(8,128)S(1)}, f32[384,1,256]{2,0,1:T(8,128)S(1)}, u32[]{:S(2)}, u32[]{:S(2)}) collective-permute-start(f32[384,1,256]{2,0,1:T(8,128)S(1)} %copy.70), channel_id=1, source_target_pairs={{1,0},{2,1},{3,2},{4,3},{5,4},{6,5},{7,6},{8,7},{9,8},{10,9},{11,1... | collective-permute-start | bytes 1179656 | tf_op jit(solution)/shard_map/ppermute | solution.py:17
  17.2 13.3 %copy-start.4 = (f32[2,16,256]{2,1,0:T(8,128)S(1)}, f32[2,16,256]{2,1,0:T(8,128)}, u32[]{:S(2)}) copy-start(f32[2,16,256]{2,1,0:T(8,128)} %param.9) | copy-start | bytes 98308
  17.2 13.3 %copy-start.7 = (s32[384,2]{0,1:T(2,128)S(1)}, s32[384,2]{0,1:T(2,128)}, u32[]{:S(2)}) copy-start(s32[384,2]{0,1:T(2,128)} %param.10) | copy-start | bytes 9220
  17.2 13.3 %copy-start.8 = (f32[8,2]{0,1:T(2,128)S(1)}, f32[8,2]{0,1:T(2,128)}, u32[]{:S(2)}) copy-start(f32[8,2]{0,1:T(2,128)} %param.11) | copy-start | bytes 196
  17.2 40.2 %collective-permute-start.1 = (f32[384,1,256]{2,0,1:T(8,128)}, f32[384,1,256]{2,0,1:T(8,128)}, u32[]{:S(2)}, u32[]{:S(2)}) collective-permute-start(f32[384,1,256]{2,0,1:T(8,128)} %copy.71), channel_id=1, source_target_pairs={{0,1},{1,2},{2,3},{3,4},{4,5},{5,6},{6,7},{7,8},{8,9},{9,10},{10,1... | collective-permute-start | bytes 1179656 | tf_op jit(solution)/shard_map/ppermute | solution.py:14
  57.2 7.5 %slice-start = ((s8[6291456]{0:T(1024)(128)(4,1)}), s8[2097152]{0:T(1024)(128)(4,1)S(1)}, s32[]{:S(2)}) async-start(s8[6291456]{0:T(1024)(128)(4,1)} %bitcast.18), calls=%async_computation.2 | async-start | bytes 4194304
  58.7 8.5 %slice-start.1 = ((s8[6291456]{0:T(1024)(128)(4,1)}), s8[4194304]{0:T(1024)(128)(4,1)S(1)}, s32[]{:S(2)}) async-start(s8[6291456]{0:T(1024)(128)(4,1)} %bitcast.18), calls=%async_computation.3 | async-start | bytes 8388608
  58.7 8.5 %copy-start.2 = (f32[384,16,255]{0,2,1:T(8,128)S(1)}, f32[384,16,255]{0,2,1:T(8,128)}, u32[]{:S(2)}) copy-start(f32[384,16,255]{0,2,1:T(8,128)} %get-tuple-element.38) | copy-start | bytes 18800644
  81.4 2.6 copy-start.1
  95.1 16.5 %collective-permute-start.4 = (f32[384,1,256]{2,0,1:T(8,128)S(1)}, f32[384,1,256]{2,0,1:T(8,128)S(1)}, u32[]{:S(2)}, u32[]{:S(2)}) collective-permute-start(f32[384,1,256]{2,0,1:T(8,128)S(1)} %copy.63), channel_id=1, source_target_pairs={{1,0},{2,1},{3,2},{4,3},{5,4},{6,5},{7,6},{8,7},{9,8},{10,9},{11,1... | collective-permute-start | bytes 1179656 | tf_op jit(solution)/shard_map/ppermute | solution.py:17
  96.5 15.2 %collective-permute-start.5 = (f32[384,1,256]{2,0,1:T(8,128)S(1)}, f32[384,1,256]{2,0,1:T(8,128)}, u32[]{:S(2)}, u32[]{:S(2)}) collective-permute-start(f32[384,1,256]{2,0,1:T(8,128)S(1)} %copy.65), channel_id=1, source_target_pairs={{0,1},{1,2},{2,3},{3,4},{4,5},{5,6},{6,7},{7,8},{8,9},{9,10},{10,1... | collective-permute-start | bytes 1179656 | tf_op jit(solution)/shard_map/ppermute | solution.py:14
  111.7 6.9 %slice-start.2 = ((s8[6291456]{0:T(1024)(128)(4,1)}), s8[2097152]{0:T(1024)(128)(4,1)S(1)}, s32[]{:S(2)}) async-start(s8[6291456]{0:T(1024)(128)(4,1)} %bitcast.20), calls=%async_computation.4 | async-start | bytes 4194304
  113.0 5.7 %slice-start.3 = ((s8[6291456]{0:T(1024)(128)(4,1)}), s8[4194304]{0:T(1024)(128)(4,1)S(1)}, s32[]{:S(2)}) async-start(s8[6291456]{0:T(1024)(128)(4,1)} %bitcast.20), calls=%async_computation.5 | async-start | bytes 8388608
  136.0 1.7 copy-start.3
  149.8 109.4 %copy-start.5 = (f32[384]{0:T(512)S(1)}, f32[384]{0:T(512)}, u32[]{:S(2)}) copy-start(f32[384]{0:T(512)} %param.15) | copy-start | bytes 4612
  149.8 109.4 %copy-start.6 = (f32[128]{0:T(128)S(1)}, f32[128]{0:T(128)}, u32[]{:S(2)}) copy-start(f32[128]{0:T(128)} %param.14) | copy-start | bytes 1540
  149.8 215.0 %all-reduce.13.cloned.1.call-start = ((), (), s32[]{:S(2)}) async-start(), calls=%async_computation.1 | async-start | bytes 6291456 | tf_op jit(solution)/shard_map/psum | solution.py:82
Sparse Core Ops, SparseCore 0:
  150.0 106.7 all-reduce.10
  261.7 103.1 all-reduce.12
where the time goes:
time: 388 us; the launch traced here: 387 us
  waiting for transfers between devices  168 us (43%)
  local copies, waits for them, and re-layouts  71.6 us (18%)
  other arithmetic  48.1 us (12%)
  matrix products  36.7 us (9%)
  blocking collectives  31 us (8%)
  starting transfers between devices  17.3 us (4%)
  between operations  14.3 us (4%)
    psum x1, waiting for transfers between devices, local(): first_pre = lax.psum(partial_first, 'grid')  107 us
    psum x1, waiting for transfers between devices, local(): back_raw = lax.psum(back_part, 'grid')  61.2 us
    slice x4, local copies, waits for them, and re-layouts, column_shift(): return jnp.concatenate([values[..., 1:], zero_col], axis=-1)  43.1 us
    psum x1, blocking collectives, local(): value = lax.psum(value_part, 'grid')  31 us
    unnamed x31, local copies, waits for them, and re-layouts  21 us
    mul x2, other arithmetic, kfe_step(): flux_y = velocity_y * centre  19.2 us
    convert_element_type x1, other arithmetic, local(): density.astype(jnp.bfloat16).reshape(scenarios, row_count * columns)  17.3 us
    dot_general x1, matrix products, local(): lax.dot_general(inputs, back_first, (((0,), (0,)), ((), ())), preferred_e...  15.5 us
  transfers between devices with their start and end apart: 8, of which 2 were waited for; matrix products, arithmetic and copies ran while one was open for 15% of the time, Pallas kernels for 0%

commit v1 on v0

--- a/solution.py
+++ b/solution.py
@@ -79,7 +79,7 @@
     back_part = lax.dot_general(
         back_second, mid_weight, (((1,), (1,)), ((), ())), preferred_element_type=jnp.float32
     )
-    back_raw = lax.psum(back_part, "grid")
+    back_raw = jnp.sum(lax.all_gather(back_part, "grid"), axis=0)
     first_f = first_act.astype(jnp.float32)
     back_first = (back_raw * (1.0 - first_f * first_f)).astype(jnp.bfloat16)
     grad_first = lax.dot_general(

time: 388 us -> 552 us (1.42)
  waiting for transfers between devices: 168 us -> 311 us
  other arithmetic: 48.1 us -> 67 us
    all_gather x0 -> x1, waiting for transfers between devices: none -> 203 us  [local(): back_raw = jnp.sum(lax.all_gather(back_part, 'grid'), axis=0)]
    psum x1 -> x0, waiting for transfers between devices: 61.2 us -> none  [local(): back_raw = lax.psum(back_part, 'grid')]
    reduce_sum x0 -> x1, other arithmetic: none -> 18.8 us  [local(): back_raw = jnp.sum(lax.all_gather(back_part, 'grid'), axis=0)]
  transfers between devices with their start and end apart: 8 -> 8, of which waited for: 2 -> 2; matrix products, arithmetic and copies ran while one was open for 15% -> 11% of each run, Pallas kernels for 0% -> 0%
where the time goes in v1:
time: 552 us; the launch traced here: 551 us
  waiting for transfers between devices  311 us (56%)
  local copies, waits for them, and re-layouts  72.7 us (13%)
  other arithmetic  67 us (12%)
  matrix products  36.7 us (7%)
  blocking collectives  32 us (6%)
  starting transfers between devices  17.2 us (3%)
  between operations  14.3 us (3%)
    all_gather x1, waiting for transfers between devices, local(): back_raw = jnp.sum(lax.all_gather(back_part, 'grid'), axis=0)  203 us
    psum x1, waiting for transfers between devices, local(): first_pre = lax.psum(partial_first, 'grid')  108 us
    slice x4, local copies, waits for them, and re-layouts, column_shift(): return jnp.concatenate([values[..., 1:], zero_col], axis=-1)  43.2 us
    psum x1, blocking collectives, local(): value = lax.psum(value_part, 'grid')  32 us
    unnamed x31, local copies, waits for them, and re-layouts  21.3 us
    mul x2, other arithmetic, kfe_step(): flux_y = velocity_y * centre  19.3 us
    reduce_sum x1, other arithmetic, local(): back_raw = jnp.sum(lax.all_gather(back_part, 'grid'), axis=0)  18.8 us
    convert_element_type x1, other arithmetic, local(): density.astype(jnp.bfloat16).reshape(scenarios, row_count * columns)  17.3 us
  transfers between devices with their start and end apart: 8, of which 2 were waited for; matrix products, arithmetic and copies ran while one was open for 11% of the time, Pallas kernels for 0%

profile of v1, /device:TPU:0, one launch (start us, length us, event | category | flops | bytes accessed | tf_op | source)
XLA Modules:
  0.0 551.1 jit_solution(6450237159370091917)
XLA Ops:
  7.2 3.4 fusion.35
  10.7 1.3 collective-permute-start
  12.8 3.8 collective-permute-start.1
  17.3 1.3 collective-permute-start.3
  18.6 4.4 collective-permute-start.2
  23.7 6.6 %copy.58 = f32[384,16,256]{0,2,1:T(8,128)} copy(f32[384,16,256]{2,1,0:T(8,128)} %param.8) | data formatting | bytes 12582912 | tf_op args[0]
  30.5 10.8 %fusion.34 = (f32[384,16,255]{0,2,1:T(8,128)}, f32[384,16,255]{0,2,1:T(8,128)}) fusion(f32[384,16,256]{0,2,1:T(8,128)} %copy.58), kind=kLoop, calls=%fused_computation.63 | loop fusion | bytes 25067520 | tf_op jit(solution)/shard_map/slice | solution.py:25
  41.3 4.9 add_multiply_fusion.1
  46.2 10.8 %fusion.36 = (f32[384,16,255]{0,2,1:T(8,128)}, f32[384,16,255]{0,2,1:T(8,128)}) fusion(f32[384,16,256]{0,2,1:T(8,128)} %add_multiply_fusion.1), kind=kLoop, calls=%fused_computation.65 | loop fusion | bytes 25067520 | tf_op jit(solution)/shard_map/slice | solution.py:25
  57.3 1.3 copy.53
  58.6 6.0 %maximum_multiply_fusion = f32[384,18,256]{0,2,1:T(8,128)} fusion(f32[384,1,256]{0,2,1:T(8,128)S(1)} %copy.51, f32[384,16,256]{0,2,1:T(8,128)} %copy.58, f32[384,1,256]{0,2,1:T(8,128)S(1)} %copy.53, f32[384]{0:T(512)S(1)} %get-tuple-element.25, f32[18,256]{1,0:T(8,128)S(1)} %fusion.20), kind=kLoop, calls=%fused_computation.1 | loop fusion | flops 7077888 | bytes 14175744 | tf_op jit(solution)/shard_map/mul | solution.py:38
  64.6 2.4 slice-done.1
  67.0 14.3 %add_multiply_fusion = (f32[384,16,256]{0,2,1:T(8,128)}, f32[384,16,256]{0,2,1:T(8,128)S(1)}) fusion(f32[384]{0:T(512)S(1)} %get-tuple-element.20, f32[16,256]{1,0:T(8,128)S(1)} %slice_bitcast_fusion, f32[384,16,255]{0,2,1:T(8,128)} %get-tuple-element.43, f32[384,16,255]{0,2,1:T(8,128)} %get-tuple-element.42, f32[384,18,256]{0,2,1:T(8,128)} %maximum_multiply_fusion, ...), kind=kLoop, calls=%fused_computation.27 | loop fusion | flops 25165824 | bytes 57329152 | tf_op jit(solution)/shard_map/mul | solution.py:40
  81.4 2.7 copy-done.1
  84.1 10.8 %fusion.31 = (f32[384,16,255]{0,2,1:T(8,128)}, f32[384,16,255]{0,2,1:T(8,128)}) fusion(f32[384,16,256]{0,2,1:T(8,128)} %copy-done.1), kind=kLoop, calls=%fused_computation.60 | loop fusion | bytes 25067520 | tf_op jit(solution)/shard_map/slice | solution.py:25
  95.0 1.3 collective-permute-start.4
  96.5 5.0 collective-permute-start.5
  101.6 10.8 %fusion.33 = (f32[384,16,255]{0,2,1:T(8,128)}, f32[384,16,255]{0,2,1:T(8,128)}) fusion(f32[384,16,256]{0,2,1:T(8,128)} %get-tuple-element.30), kind=kLoop, calls=%fused_computation.62 | loop fusion | bytes 25067520 | tf_op jit(solution)/shard_map/slice | solution.py:25
  112.6 1.3 copy.66
  113.9 5.5 %maximum_multiply_fusion.1 = f32[384,18,256]{0,2,1:T(8,128)} fusion(f32[384,1,256]{0,2,1:T(8,128)S(1)} %copy.64, f32[384,16,256]{0,2,1:T(8,128)} %copy-done.1, f32[384,1,256]{0,2,1:T(8,128)S(1)} %copy.66, f32[384]{0:T(512)S(1)} %get-tuple-element.21, f32[18,256]{1,0:T(8,128)S(1)} %fusion.20), kind=kLoop, calls=%fused_computation.2 | loop fusion | flops 7077888 | bytes 14175744 | tf_op jit(solution)/shard_map/mul | solution.py:38
  119.5 17.3 %fusion.28 = (bf16[384,16,256]{0,2,1:T(8,128)(2,1)S(1)}, f32[384,16,256]{0,2,1:T(8,128)}) fusion(f32[384,16,255]{0,2,1:T(8,128)} %get-tuple-element.37, f32[384,16,255]{0,2,1:T(8,128)} %get-tuple-element.36, f32[384,18,256]{0,2,1:T(8,128)} %maximum_multiply_fusion.1, f32[384,16,256]{0,2,1:T(8,128)S(1)} %bitcast.22, f32[384,16,255]{0,2,1:T(8,128)} %get-tuple-element.33, ...), kind=kLoop, calls=%fused_computation.59 | loop fusion | flops 23592960 | bytes 54165504 | tf_op jit(solution)/shard_map/convert_element_type | solution.py:63
  136.8 1.6 copy-done.3
  138.4 12.1 %fusion.38 = f32[384,2048]{1,0:T(8,128)} fusion(bf16[384,4096]{0,1:T(8,128)(2,1)S(1)} %bitcast.24, bf16[4096,2048]{1,0:T(8,128)(2,1)} %param.12), kind=kOutput, calls=%fused_computation.67 | convolution fusion | flops 6442450944 | bytes 23068672 | tf_op jit(solution)/shard_map/dot_general | solution.py:64
  150.6 107.8 %all-reduce.10.cloned.1.call-done = f32[384,2048]{1,0:T(8,128)} async-done(((f32[384,2048]{1,0:T(8,128)}), f32[384,2048]{1,0:T(8,128)}) %all-reduce.10.cloned.1.call-update) | async-done | bytes 3145744 | tf_op jit(solution)/shard_map/psum | solution.py:65
  258.5 2.5 fusion.19
  261.0 2.3 fusion.23
  263.3 7.0 %copy.69 = f32[384,16,256]{2,1,0:T(8,128)} copy(f32[384,16,256]{0,2,1:T(8,128)} %get-tuple-element.29) | data formatting | bytes 12582912
  270.5 32.0 %psum.15 = f32[384]{0:T(512)} all-reduce(f32[384]{0:T(512)S(1)} %convolution_reduce_fusion), channel_id=1, replica_groups=mesh['groups'=2,'grid'=16] {'grid'}, use_global_device_ids=true, to_apply=%region_3.0 | all-reduce | flops 384 | bytes 3072 | tf_op jit(solution)/shard_map/psum | solution.py:71
  303.2 3.4 convolution_convert_fusion.1
  306.6 203.4 %all-gather.3.cloned.1.call-done = f32[6144,2048]{1,0:T(8,128)} async-done(((f32[384,2048]{1,0:T(8,128)}), f32[6144,2048]{1,0:T(8,128)}) %all-gather.3.cloned.1.call-update) | async-done | bytes 50331664 | tf_op jit(solution)/shard_map/all_gather | solution.py:82
  510.0 18.8 %reduce_sum.29 = f32[384,2048]{1,0:T(8,128)} reduce(f32[16,384,2048]{2,1,0:T(8,128)} %bitcast.23, f32[]{:T(128)} %constant.5.clone.1), dimensions={0}, to_apply=%region_4.0 | reduce | flops 11796480 | bytes 53477380 | tf_op jit(solution)/shard_map/reduce_sum | solution.py:82
  528.8 15.5 %convolution_convert_fusion = bf16[4096,2048]{1,0:T(8,128)(2,1)} fusion(bf16[384,4096]{0,1:T(8,128)(2,1)} %bitcast.25, f32[384,2048]{1,0:T(8,128)} %reduce_sum.29, f32[384,2048]{1,0:T(8,128)} %all-reduce.10.cloned.1.call-done), kind=kOutput, calls=%fused_computation | convolution fusion | flops 6455558144 | bytes 26214400 | tf_op jit(solution)/shard_map/dot_general | solution.py:85
  (53 shorter events, 4.3 us)
Async XLA Ops:
  7.2 251.3 %copy-start = (bf16[2048,128]{1,0:T(8,128)(2,1)S(1)}, bf16[2048,128]{1,0:T(8,128)(2,1)}, u32[]{:S(2)}) copy-start(bf16[2048,128]{1,0:T(8,128)(2,1)} %param.13) | copy-start | bytes 1572868
  7.2 251.3 %all-reduce.10.cloned.1.call-start = ((), (), s32[]{:S(2)}) async-start(), calls=%async_computation | async-start | bytes 6291456 | tf_op jit(solution)/shard_map/psum | solution.py:65
  10.7 46.4 %collective-permute-start = (f32[384,1,256]{2,0,1:T(8,128)S(1)}, f32[384,1,256]{2,0,1:T(8,128)S(1)}, u32[]{:S(2)}, u32[]{:S(2)}) collective-permute-start(f32[384,1,256]{2,0,1:T(8,128)S(1)} %copy.70), channel_id=1, source_target_pairs={{1,0},{2,1},{3,2},{4,3},{5,4},{6,5},{7,6},{8,7},{9,8},{10,9},{11,1... | collective-permute-start | bytes 1179656 | tf_op jit(solution)/shard_map/ppermute | solution.py:17
  12.8 44.5 %collective-permute-start.1 = (f32[384,1,256]{2,0,1:T(8,128)}, f32[384,1,256]{2,0,1:T(8,128)}, u32[]{:S(2)}, u32[]{:S(2)}) collective-permute-start(f32[384,1,256]{2,0,1:T(8,128)} %copy.71), channel_id=1, source_target_pairs={{0,1},{1,2},{2,3},{3,4},{4,5},{5,6},{6,7},{7,8},{8,9},{9,10},{10,1... | collective-permute-start | bytes 1179656 | tf_op jit(solution)/shard_map/ppermute | solution.py:14
  17.3 39.7 %collective-permute-start.3 = (f32[2,1,256]{2,1,0:T(1,128)S(1)}, f32[2,1,256]{2,1,0:T(1,128)S(1)}, u32[]{:S(2)}, u32[]{:S(2)}) collective-permute-start(f32[2,1,256]{2,1,0:T(1,128)S(1)} %get-tuple-element.45), channel_id=1, source_target_pairs={{1,0},{2,1},{3,2},{4,3},{5,4},{6,5},{7,6},{8,7},{9,8},{10,9},{11,1... | collective-permute-start | bytes 6152 | tf_op jit(solution)/shard_map/ppermute | solution.py:17
  18.6 38.4 %collective-permute-start.2 = (f32[2,1,256]{2,1,0:T(1,128)S(1)}, f32[2,1,256]{2,1,0:T(1,128)S(1)}, u32[]{:S(2)}, u32[]{:S(2)}) collective-permute-start(f32[2,1,256]{2,1,0:T(1,128)S(1)} %get-tuple-element.44), channel_id=1, source_target_pairs={{0,1},{1,2},{2,3},{3,4},{4,5},{5,6},{6,7},{7,8},{8,9},{9,10},{10,1... | collective-permute-start | bytes 6152 | tf_op jit(solution)/shard_map/ppermute | solution.py:14
  23.7 6.6 %copy-start.7 = (s32[384,2]{0,1:T(2,128)S(1)}, s32[384,2]{0,1:T(2,128)}, u32[]{:S(2)}) copy-start(s32[384,2]{0,1:T(2,128)} %param.10) | copy-start | bytes 9220
  23.7 6.6 %copy-start.8 = (f32[8,2]{0,1:T(2,128)S(1)}, f32[8,2]{0,1:T(2,128)}, u32[]{:S(2)}) copy-start(f32[8,2]{0,1:T(2,128)} %param.11) | copy-start | bytes 196
  46.2 10.8 %copy-start.4 = (f32[2,16,256]{2,1,0:T(8,128)S(1)}, f32[2,16,256]{2,1,0:T(8,128)}, u32[]{:S(2)}) copy-start(f32[2,16,256]{2,1,0:T(8,128)} %param.9) | copy-start | bytes 98308
  57.1 7.5 %slice-start = ((s8[6291456]{0:T(1024)(128)(4,1)}), s8[2097152]{0:T(1024)(128)(4,1)S(1)}, s32[]{:S(2)}) async-start(s8[6291456]{0:T(1024)(128)(4,1)} %bitcast.19), calls=%async_computation.2 | async-start | bytes 4194304
  58.5 8.5 %slice-start.1 = ((s8[6291456]{0:T(1024)(128)(4,1)}), s8[4194304]{0:T(1024)(128)(4,1)S(1)}, s32[]{:S(2)}) async-start(s8[6291456]{0:T(1024)(128)(4,1)} %bitcast.19), calls=%async_computation.3 | async-start | bytes 8388608
  58.5 8.5 %copy-start.2 = (f32[384,16,255]{0,2,1:T(8,128)S(1)}, f32[384,16,255]{0,2,1:T(8,128)}, u32[]{:S(2)}) copy-start(f32[384,16,255]{0,2,1:T(8,128)} %get-tuple-element.38) | copy-start | bytes 18800644
  81.4 2.7 copy-start.1
  95.0 17.3 %collective-permute-start.4 = (f32[384,1,256]{2,0,1:T(8,128)S(1)}, f32[384,1,256]{2,0,1:T(8,128)S(1)}, u32[]{:S(2)}, u32[]{:S(2)}) collective-permute-start(f32[384,1,256]{2,0,1:T(8,128)S(1)} %copy.63), channel_id=1, source_target_pairs={{1,0},{2,1},{3,2},{4,3},{5,4},{6,5},{7,6},{8,7},{9,8},{10,9},{11,1... | collective-permute-start | bytes 1179656 | tf_op jit(solution)/shard_map/ppermute | solution.py:17
  96.5 16.0 %collective-permute-start.5 = (f32[384,1,256]{2,0,1:T(8,128)S(1)}, f32[384,1,256]{2,0,1:T(8,128)}, u32[]{:S(2)}, u32[]{:S(2)}) collective-permute-start(f32[384,1,256]{2,0,1:T(8,128)S(1)} %copy.65), channel_id=1, source_target_pairs={{0,1},{1,2},{2,3},{3,4},{4,5},{5,6},{6,7},{7,8},{8,9},{9,10},{10,1... | collective-permute-start | bytes 1179656 | tf_op jit(solution)/shard_map/ppermute | solution.py:14
  112.5 6.9 %slice-start.2 = ((s8[6291456]{0:T(1024)(128)(4,1)}), s8[2097152]{0:T(1024)(128)(4,1)S(1)}, s32[]{:S(2)}) async-start(s8[6291456]{0:T(1024)(128)(4,1)} %bitcast.21), calls=%async_computation.4 | async-start | bytes 4194304
  113.9 5.7 %slice-start.3 = ((s8[6291456]{0:T(1024)(128)(4,1)}), s8[4194304]{0:T(1024)(128)(4,1)S(1)}, s32[]{:S(2)}) async-start(s8[6291456]{0:T(1024)(128)(4,1)} %bitcast.21), calls=%async_computation.5 | async-start | bytes 8388608
  136.8 1.6 copy-start.3
  150.5 110.4 %copy-start.5 = (f32[384]{0:T(512)S(1)}, f32[384]{0:T(512)}, u32[]{:S(2)}) copy-start(f32[384]{0:T(512)} %param.15) | copy-start | bytes 4612
  150.5 110.4 %copy-start.6 = (f32[128]{0:T(128)S(1)}, f32[128]{0:T(128)}, u32[]{:S(2)}) copy-start(f32[128]{0:T(128)} %param.14) | copy-start | bytes 1540
  150.6 359.4 %all-gather.3.cloned.1.call-start = ((), (), s32[]{:S(2)}) async-start(), calls=%async_computation.1 | async-start | bytes 53477376 | tf_op jit(solution)/shard_map/all_gather | solution.py:82
Sparse Core Ops, SparseCore 0:
  150.7 107.7 all-reduce.9
  263.4 246.5 all-gather.2
